TPU v7x, 256 devices: a whole 4x4x8 slice. The times are simulated.
256 devices in a mesh: section: 16 (over y_hi, x, core), ray: 8 (over z), dp: 2 (over y_lo).
Axes of the slice: x: 4, y: 4 (y_hi: 2, y_lo: 2; y = y_hi * 2 + y_lo), z: 8, core: 2. Of those that a mesh axis runs over, the one named last changes fastest.
Arguments:
- section_tokens: bfloat16 [16, 2, 1024, 1024], P('section', 'dp', 'ray'), may hold values from -6 to 6
- enc_ln1: float32 [16, 1024], P('section'), may hold values from 0.5 to 1.5
- enc_qkv: bfloat16 [16, 1024, 3, 1024], P('section', None, None, 'ray'), may hold values from -40 to 40
- enc_out: bfloat16 [16, 1024, 1024], P('section', 'ray'), may hold values from -0.1875 to 0.1875
- enc_ln2: float32 [16, 1024], P('section'), may hold values from 0.5 to 1.5
- enc_up: bfloat16 [16, 1024, 4096], P('section', None, 'ray'), may hold values from -0.1875 to 0.1875
- enc_down: bfloat16 [16, 4096, 1024], P('section', 'ray'), may hold values from -0.09375 to 0.09375
- set_latent: bfloat16 [2, 1024, 1024], P('dp', 'ray'), may hold values from -6 to 6
- ray_queries: bfloat16 [2, 32768, 1024], P('dp', ('section', 'ray')), may hold values from -6 to 6
- dec_query: bfloat16 [1024, 1024], P('section'), may hold values from -40 to 40
- dec_kv: bfloat16 [1024, 2, 1024], P('section'), may hold values from -1 to 1
- dec_out: bfloat16 [1024, 1024], P('section'), may hold values from -0.1875 to 0.1875
- feature_grad: bfloat16 [2, 32768, 1024], P('dp', ('section', 'ray')), may hold values from -2 to 2
Outputs:
- handed: bfloat16 [16, 2, 1024, 1024], P('section', 'dp', 'ray')
- finished: bfloat16 [2, 1024, 1024], P('dp', 'ray', 'section')
- ray_features: bfloat16 [2, 32768, 1024], P('dp', ('section', 'ray'))
- latent_grad: bfloat16 [2, 1024, 1024], P('dp', 'ray')
- out_grad: float32 [1024, 1024], replicated
All inputs are finite; a program needn't handle non-finite values.
Results may differ from a plain program's by a relative error of at most 0.022.
The roundings to bfloat16 on the way count: a program that leaves them out, or rounds other values in their place, can miss the bound.
Values may be sent and summed in bfloat16 or wider, within the bound.
No kernel may reach another device: no remote copies, remote signals or barrier semaphores. Data moves between devices by JAX's collectives and lax.ppermute only.
A program may use at most 128 MiB of HBM per device.

v0:
```python
import math
import jax
import jax.numpy as jnp
from jax import lax
from jax.sharding import PartitionSpec as P

HEADS = 16


def shifted(value, axis, by):
    count = lax.axis_size(axis)
    pairs = [(i, i + by) for i in range(count) if 0 <= i + by < count]
    return lax.ppermute(value, axis, pairs)


def spread_2(value, axis, root):
    mine = lax.axis_index(axis) == root
    return lax.psum(jnp.where(mine, value, jnp.zeros_like(value)), axis)


def layer_norm(values, gain):
    values = values.astype(jnp.float32)
    center = values - jnp.mean(values, -1, keepdims=True)
    spread = jnp.mean(center * center, -1, keepdims=True)
    return center * lax.rsqrt(spread + 1e-05) * gain


def softmax_rows(scores):
    top = jnp.max(scores, -1, keepdims=True)
    expo = jnp.exp(scores - top)
    return expo / jnp.sum(expo, -1, keepdims=True)


def attend_heads(packed, head_dim):
    length = packed.shape[0]
    heads = packed.shape[1] // (3 * head_dim)
    split = packed.reshape(length, 3, heads, head_dim)
    scores = jnp.einsum(
        "qhd,khd->hqk", split[:, 0], split[:, 1], preferred_element_type=jnp.float32
    ) / math.sqrt(head_dim)
    probs = softmax_rows(scores).astype(jnp.bfloat16)
    mixed = jnp.einsum("hqk,khd->qhd", probs, split[:, 2], preferred_element_type=jnp.float32)
    return mixed.astype(jnp.bfloat16).reshape(length, heads * head_dim)


def latent_rows(pair_sum, w_pairs):
    result = lax.dot_general(
        pair_sum[:, 0],
        w_pairs[:, 0, :],
        (((1,), (1,)), ((), ())),
        preferred_element_type=jnp.float32,
    )
    result = result + lax.dot_general(
        pair_sum[:, 1],
        w_pairs[:, 1, :],
        (((1,), (1,)), ((), ())),
        preferred_element_type=jnp.float32,
    )
    return result.astype(jnp.bfloat16)


def local(
    section_tokens,
    enc_ln1,
    enc_qkv,
    enc_out,
    enc_ln2,
    enc_up,
    enc_down,
    set_latent,
    ray_queries,
    dec_query,
    dec_kv,
    dec_out,
    feature_grad,
):
    tokens = section_tokens[0, 0]
    width = tokens.shape[1]
    head_dim = width // HEADS
    local_width = enc_out.shape[1]
    w_qkv = enc_qkv[0].reshape(width, 3 * local_width)
    w_attn_out = enc_out[0]
    w_upper = enc_up[0]
    w_lower = enc_down[0]
    gain_one = enc_ln1[0]
    gain_two = enc_ln2[0]
    normed = layer_norm(tokens, gain_one).astype(jnp.bfloat16)
    packed = jnp.dot(
        lax.all_gather(normed, "ray", axis=0, tiled=True), w_qkv, preferred_element_type=jnp.float32
    ).astype(jnp.bfloat16)
    mixed = attend_heads(packed, head_dim)
    attn_rows = lax.psum_scatter(
        jnp.dot(mixed, w_attn_out, preferred_element_type=jnp.float32).astype(jnp.bfloat16),
        "ray",
        scatter_dimension=0,
        tiled=True,
    ).astype(jnp.float32)
    hidden = (tokens.astype(jnp.float32) + attn_rows).astype(jnp.bfloat16)
    upper = jax.nn.gelu(
        jnp.dot(
            lax.all_gather(
                layer_norm(hidden, gain_two).astype(jnp.bfloat16), "ray", axis=0, tiled=True
            ),
            w_upper,
            preferred_element_type=jnp.float32,
        ),
        approximate=True,
    ).astype(jnp.bfloat16)
    lower_rows = lax.psum_scatter(
        jnp.dot(upper, w_lower, preferred_element_type=jnp.float32).astype(jnp.bfloat16),
        "ray",
        scatter_dimension=0,
        tiled=True,
    ).astype(jnp.float32)
    layer_out = (hidden.astype(jnp.float32) + lower_rows).astype(jnp.bfloat16)
    handed = shifted(layer_out, "section", 1)
    finished_all = spread_2(layer_out, "section", lax.axis_size("section") - 1)
    columns = width // lax.axis_size("section")
    finished = lax.dynamic_slice_in_dim(
        finished_all, lax.axis_index("section") * columns, columns, 1
    )
    w_query, w_pairs, w_mix = (
        lax.all_gather(dec_query, "section", axis=0, tiled=True),
        lax.all_gather(dec_kv, "section", axis=0, tiled=True),
        lax.all_gather(dec_out, "section", axis=0, tiled=True),
    )
    latent = set_latent[0]
    queries = ray_queries[0]
    cotangent = feature_grad[0]
    flat_pairs = w_pairs.reshape(width, 2 * width)
    key_values = lax.all_gather(
        jnp.dot(latent, flat_pairs, preferred_element_type=jnp.float32).astype(jnp.bfloat16),
        "ray",
        axis=0,
        tiled=True,
    )
    scene_len = key_values.shape[0]
    ray_rows = queries.shape[0]
    scale = 1.0 / math.sqrt(head_dim)
    keys = key_values[:, :width].reshape(scene_len, HEADS, head_dim)
    values = key_values[:, width:].reshape(scene_len, HEADS, head_dim)
    query = (
        jnp.dot(queries, w_query, preferred_element_type=jnp.float32)
        .astype(jnp.bfloat16)
        .reshape(ray_rows, HEADS, head_dim)
    )
    scores = jnp.einsum("rhd,lhd->hrl", query, keys, preferred_element_type=jnp.float32) * scale
    probs = softmax_rows(scores)
    probs_low = probs.astype(jnp.bfloat16)
    attended = (
        jnp.einsum("hrl,lhd->rhd", probs_low, values, preferred_element_type=jnp.float32)
        .astype(jnp.bfloat16)
        .reshape(ray_rows, width)
    )
    features = (
        queries.astype(jnp.float32) + jnp.dot(attended, w_mix, preferred_element_type=jnp.float32)
    ).astype(jnp.bfloat16)
    mix_term = lax.dot_general(
        attended, cotangent, (((0,), (0,)), ((), ())), preferred_element_type=jnp.float32
    )
    out_grad = lax.psum(mix_term, ("section", "ray", "dp"))
    attn_grad = lax.dot_general(
        cotangent, w_mix, (((1,), (1,)), ((), ())), preferred_element_type=jnp.float32
    )
    attn_grad = attn_grad.astype(jnp.bfloat16).reshape(ray_rows, HEADS, head_dim)
    prob_grad = jnp.einsum("rhd,lhd->hrl", attn_grad, values, preferred_element_type=jnp.float32)
    delta = jnp.sum(probs * prob_grad, -1, keepdims=True)
    score_grad = (probs * (prob_grad - delta) * scale).astype(jnp.bfloat16)
    count = latent.shape[0] * lax.axis_size("ray")
    key_grad = jnp.einsum(
        "hrl,rhd->lhd", score_grad, query, preferred_element_type=jnp.float32
    ).reshape(count, width)
    value_grad = jnp.einsum(
        "hrl,rhd->lhd", probs_low, attn_grad, preferred_element_type=jnp.float32
    ).reshape(count, width)
    stacked = jnp.stack([key_grad, value_grad], 1)
    pair_rows = lax.psum_scatter(
        stacked.astype(jnp.bfloat16), "ray", scatter_dimension=0, tiled=True
    )
    pair_sum = lax.psum(pair_rows, "section")
    latent_grad = latent_rows(pair_sum, w_pairs)
    return (handed[None, None], finished[None], features[None], latent_grad[None], out_grad)


def solution(mesh):
    return jax.shard_map(
        local,
        mesh=mesh,
        in_specs=(
            P("section", "dp", "ray", None),
            P("section", None),
            P("section", None, None, "ray"),
            P("section", "ray", None),
            P("section", None),
            P("section", None, "ray"),
            P("section", "ray", None),
            P("dp", "ray", None),
            P("dp", ("section", "ray"), None),
            P("section", None),
            P("section", None, None),
            P("section", None),
            P("dp", ("section", "ray"), None),
        ),
        out_specs=(
            P("section", "dp", "ray", None),
            P("dp", "ray", "section"),
            P("dp", ("section", "ray"), None),
            P("dp", "ray", None),
            P(),
        ),
        check_vma=False,
    )
```

profile of v0, /device:TPU:2, one launch (start us, length us, event | category | flops | bytes accessed | tf_op | source)
XLA Modules:
  0.0 928.3 jit_solution(4946242236666145838)
XLA Ops:
  13.8 42.5 %all-gather.7.cloned.1.call-done = bf16[1024,1024]{1,0:T(8,128)(2,1)} async-done(((bf16[128,1024]{1,0:T(8,128)(2,1)}), bf16[1024,1024]{1,0:T(8,128)(2,1)}) %all-gather.7.cloned.1.call-update) | async-done | bytes 2097168 | tf_op jit(solution)/shard_map/all_gather | solution.py:89
  56.3 2.6 convolution_convert_fusion.3
  58.9 4.9 fusion.97
  63.7 4.3 fusion.48
  71.9 39.7 %reduce-scatter.6.cloned.1.call-done = bf16[128,1024]{1,0:T(8,128)(2,1)} async-done(((bf16[1024,1024]{1,0:T(8,128)(2,1)}), bf16[128,1024]{1,0:T(8,128)(2,1)}) %reduce-scatter.6.cloned.1.call-update) | async-done | bytes 262160 | tf_op jit(solution)/shard_map/reduce_scatter | solution.py:92
  114.0 18.6 %all-gather.11.cloned.1.call-done = bf16[1024,2,1024]{2,1,0:T(2,128)(2,1)} async-done(((bf16[64,2,1024]{2,1,0:T(2,128)(2,1)}), bf16[1024,2,1024]{2,1,0:T(2,128)(2,1)}) %all-gather.11.cloned.1.call-update) | async-done | bytes 4194320 | tf_op jit(solution)/shard_map/all_gather | solution.py:124
  132.7 11.1 %copy.47 = bf16[1024,2,1024]{0,2,1:T(8,128)(2,1)} copy(bf16[1024,2,1024]{2,1,0:T(2,128)(2,1)} %all-gather.11.cloned.1.call-done) | data formatting | bytes 8388608 | tf_op jit(solution)/shard_map/all_gather | solution.py:124
  143.8 4.6 convolution_convert_fusion
  148.5 39.0 %all-gather.15.cloned.1.call-done = bf16[1024,1024]{1,0:T(8,128)(2,1)} async-done(((bf16[64,1024]{1,0:T(8,128)(2,1)}), bf16[1024,1024]{1,0:T(8,128)(2,1)}) %all-gather.15.cloned.1.call-update) | async-done | bytes 2097168 | tf_op jit(solution)/shard_map/all_gather | solution.py:123
  190.8 51.5 %all-gather.17.cloned.1.call-done = bf16[1024,1024]{1,0:T(8,128)(2,1)} async-done(((bf16[64,1024]{1,0:T(8,128)(2,1)}), bf16[1024,1024]{1,0:T(8,128)(2,1)}) %all-gather.17.cloned.1.call-update) | async-done | bytes 2097168 | tf_op jit(solution)/shard_map/all_gather | solution.py:125
  245.6 39.2 %all-gather.9.cloned.1.call-done = bf16[1024,1024]{1,0:T(8,128)(2,1)} async-done(((bf16[128,1024]{1,0:T(8,128)(2,1)}), bf16[1024,1024]{1,0:T(8,128)(2,1)}) %all-gather.9.cloned.1.call-update) | async-done | bytes 2097168 | tf_op jit(solution)/shard_map/all_gather | solution.py:101
  284.9 5.8 convolution_convert_fusion.1
  290.9 66.2 %all-gather.13.cloned.1.call-done = bf16[1024,2048]{1,0:T(8,128)(2,1)} async-done(((bf16[128,2048]{1,0:T(8,128)(2,1)}), bf16[1024,2048]{1,0:T(8,128)(2,1)}) %all-gather.13.cloned.1.call-update) | async-done | bytes 4194320 | tf_op jit(solution)/shard_map/all_gather | solution.py:131
  357.2 4.0 fusion.96
  361.2 2.6 copy.50
  363.8 2.9 copy.48
  366.7 9.8 %fusion.98 = (f32[16,256]{1,0:T(8,128)S(1)}, f32[16,256,1024]{2,1,0:T(8,128)}) fusion(bf16[256,16,64]{0,2,1:T(8,128)(2,1)S(1)} %bitcast.149, bf16[1024,16,64]{0,2,1:T(8,128)(2,1)} %bitcast.144), kind=kOutput, calls=%fused_computation.110 | convolution fusion | flops 549454848 | bytes 19415040 | tf_op jit(solution)/shard_map/sub | solution.py:30
  376.5 8.1 fusion.99
  384.5 38.2 %fusion.38 = bf16[16,64,1024]{2,1,0:T(8,128)(2,1)} fusion(bf16[256,16,64]{0,2,1:T(8,128)(2,1)S(1)} %bitcast.150, f32[16,256,1024]{2,1,0:T(8,128)} %fusion.99, f32[16,256,1024]{2,1,0:T(8,128)} %get-tuple-element.18, f32[16,256]{1,0:T(8,128)S(1)} %get-tuple-element.17), kind=kOutput, calls=%fused_computation.40 | convolution fusion | flops 567284736 | bytes 36192256 | tf_op jit(solution)/shard_map/hrl,rhd->lhd/dot_general | solution.py:170
  422.8 7.1 fusion.35
  429.9 2.4 pad_maximum_fusion
  432.3 6.5 copy.57
  440.8 52.2 %reduce-scatter.10.cloned.1.call-done = bf16[128,2048]{1,0:T(8,128)(2,1)} async-done(((bf16[1024,2048]{1,0:T(8,128)(2,1)}), bf16[128,2048]{1,0:T(8,128)(2,1)}) %reduce-scatter.10.cloned.1.call-update) | async-done | bytes 524304
  495.3 8.5 fusion.42
  503.8 2.7 fusion.78
  506.5 10.0 %fusion.95 = (bf16[1024,1,1024]{2,1,0:T(2,128)(2,1)}, bf16[1024,1,1024]{2,1,0:T(2,128)(2,1)}) fusion(bf16[1024,2,1024]{2,1,0:T(2,128)(2,1)} %all-gather.11.cloned.1.call-done), kind=kLoop, calls=%fused_computation.107 | loop fusion | bytes 8388608 | tf_op jit(solution)/shard_map/slice | solution.py:49
  520.0 4.7 collective-permute-done
  524.7 109.9 %all-reduce.6.cloned.1.call-done = (bf16[128,1024]{1,0:T(8,128)(2,1)}, bf16[128,2,1024]{0,2,1:T(8,128)(2,1)}) async-done(((bf16[128,1024]{1,0:T(8,128)(2,1)}, bf16[128,2,1024]{0,2,1:T(8,128)(2,1)}), (bf16[128,1024]{1,0:T(8,128)(2,1)}, bf16[128,2,1024]{0,2,1:T(8,128)(2,1)})) %all-reduce.6.cloned.1.call-update) | async-done | bytes 786448 | tf_op jit(solution)/shard_map/psum | solution.py:18
  636.2 3.1 fusion.33
  639.3 3.9 fusion.49
  643.2 272.5 %all-reduce.4.cloned.1.call-done = f32[1024,1024]{1,0:T(8,128)} async-done(((f32[1024,1024]{1,0:T(8,128)}), f32[1024,1024]{1,0:T(8,128)}) %all-reduce.4.cloned.1.call-update) | async-done | bytes 4194320 | tf_op jit(solution)/shard_map/psum | solution.py:161
  916.4 4.8 copy.76
  (76 shorter events, 28.8 us)
Async XLA Ops:
  8.0 276.9 %copy-start = (bf16[1,512,1024]{2,1,0:T(8,128)(2,1)S(1)}, bf16[1,512,1024]{2,1,0:T(8,128)(2,1)}, u32[]{:S(2)}) copy-start(bf16[1,512,1024]{2,1,0:T(8,128)(2,1)} %param.19) | copy-start | bytes 3145732
  8.0 48.2 %all-gather.7.cloned.1.call-start = ((), (), s32[]{:S(2)}) async-start(), calls=%async_computation.3 | async-start | bytes 2359296 | tf_op jit(solution)/shard_map/all_gather | solution.py:89
  12.3 99.4 %reduce-scatter.6.cloned.1.call-start = ((), (), s32[]{:S(2)}) async-start(), calls=%async_computation.4 | async-start | bytes 2359296 | tf_op jit(solution)/shard_map/reduce_scatter | solution.py:92
  63.7 4.3 copy-start.11
  68.0 43.6 %copy-start.2 = (bf16[1,1,128,1024]{3,2,1,0:T(8,128)(2,1)S(1)}, bf16[1,1,128,1024]{3,2,1,0:T(8,128)(2,1)}, u32[]{:S(2)}) copy-start(bf16[1,1,128,1024]{3,2,1,0:T(8,128)(2,1)} %param.13) | copy-start | bytes 786436
  68.0 45.0 %copy-start.14 = (f32[1,1024]{1,0:T(1,128)S(1)}, f32[1,1024]{1,0:T(1,128)}, u32[]{:S(2)}) copy-start(f32[1,1024]{1,0:T(1,128)} %param.17) | copy-start | bytes 12292
  70.1 62.5 %all-gather.11.cloned.1.call-start = ((), (), s32[]{:S(2)}) async-start(), calls=%async_computation.7 | async-start | bytes 4456448 | tf_op jit(solution)/shard_map/all_gather | solution.py:124
  70.7 116.8 %all-gather.15.cloned.1.call-start = ((), (), s32[]{:S(2)}) async-start(), calls=%async_computation.9 | async-start | bytes 2228224 | tf_op jit(solution)/shard_map/all_gather | solution.py:123
  71.3 171.0 %all-gather.17.cloned.1.call-start = ((), (), s32[]{:S(2)}) async-start(), calls=%async_computation.10 | async-start | bytes 2228224 | tf_op jit(solution)/shard_map/all_gather | solution.py:125
  71.9 213.0 %all-gather.9.cloned.1.call-start = ((), (), s32[]{:S(2)}) async-start(), calls=%async_computation.5 | async-start | bytes 2359296 | tf_op jit(solution)/shard_map/all_gather | solution.py:101
  114.0 29.8 %copy-start.12 = (bf16[1,128,1024]{2,1,0:T(8,128)(2,1)S(1)}, bf16[1,128,1024]{2,1,0:T(8,128)(2,1)}, u32[]{:S(2)}) copy-start(bf16[1,128,1024]{2,1,0:T(8,128)(2,1)} %param.20) | copy-start | bytes 786436
  114.0 243.2 %all-gather.13.cloned.1.call-start = ((), (), s32[]{:S(2)}) async-start(), calls=%async_computation.8 | async-start | bytes 4718592 | tf_op jit(solution)/shard_map/all_gather | solution.py:131
  143.8 43.7 %copy-start.8 = (bf16[1,256,1024]{2,1,0:T(8,128)(2,1)S(1)}, bf16[1,256,1024]{2,1,0:T(8,128)(2,1)}, u32[]{:S(2)}) copy-start(bf16[1,256,1024]{2,1,0:T(8,128)(2,1)} %param.21) | copy-start | bytes 1572868
  143.8 98.5 %copy-start.6 = (bf16[1,256,1024]{2,1,0:T(8,128)(2,1)S(1)}, bf16[1,256,1024]{2,1,0:T(8,128)(2,1)}, u32[]{:S(2)}) copy-start(bf16[1,256,1024]{2,1,0:T(8,128)(2,1)} %param.25) | copy-start | bytes 1572868
  148.5 290.5 %reduce-scatter.8.cloned.1.call-start = ((), (), s32[]{:S(2)}) async-start(), calls=%async_computation.6 | async-start | bytes 2359296 | tf_op jit(solution)/shard_map/reduce_scatter | solution.py:109
  290.7 202.2 %reduce-scatter.10.cloned.1.call-start = ((), (), s32[]{:S(2)}) async-start(), calls=%async_computation.12 | async-start | bytes 4718592
  361.2 5.4 copy-start.10
  366.6 9.8 %copy-start.4 = (bf16[256,1024]{0,1:T(8,128)(2,1)S(1)}, bf16[256,1024]{0,1:T(8,128)(2,1)}, u32[]{:S(2)}) copy-start(bf16[256,1024]{0,1:T(8,128)(2,1)} %copy.51) | copy-start | bytes 1572868
  422.8 7.1 copy-start.5
  438.8 195.8 %all-reduce.6.cloned.1.call-start = ((), (), s32[]{:S(2)}) async-start(), calls=%async_computation.13 | async-start | bytes 1572864 | tf_op jit(solution)/shard_map/psum | solution.py:18
  495.0 8.8 copy-start.7
  495.0 420.7 %all-reduce.4.cloned.1.call-start = ((), (), s32[]{:S(2)}) async-start(), calls=%async_computation.11 | async-start | bytes 8388608 | tf_op jit(solution)/shard_map/psum | solution.py:161
  506.5 10.0 %copy-start.13 = (bf16[128,1024]{1,0:T(8,128)(2,1)S(1)}, bf16[128,1024]{1,0:T(8,128)(2,1)}, u32[]{:S(2)}) copy-start(bf16[128,1024]{1,0:T(8,128)(2,1)} %get-tuple-element.8) | copy-start | bytes 786436
  506.5 11.9 %copy-start.3 = (bf16[1024,1024]{1,0:T(8,128)(2,1)S(1)}, bf16[1024,1024]{1,0:T(8,128)(2,1)}, u32[]{:S(2)}) copy-start(bf16[1024,1024]{1,0:T(8,128)(2,1)} %all-gather.17.cloned.1.call-done) | copy-start | bytes 6291460
  506.5 11.9 %copy-start.9 = (bf16[1,256,1024]{2,1,0:T(8,128)(2,1)S(1)}, bf16[1,256,1024]{2,1,0:T(8,128)(2,1)}, u32[]{:S(2)}) copy-start(bf16[1,256,1024]{2,1,0:T(8,128)(2,1)} %param.21) | copy-start | bytes 1572868
  516.5 8.2 collective-permute-start
  915.7 5.5 copy-start.1
Sparse Core Ops, SparseCore 0:
  12.4 43.7 all-gather.6
  70.3 41.3 reduce-scatter.5
  290.8 69.1 reduce-scatter.7
  439.0 53.9 reduce-scatter.9
Sparse Core Ops, SparseCore 1:
  73.4 59.3 all-gather.10
  135.3 52.1 all-gather.14
  190.1 52.1 all-gather.16
  244.7 40.1 all-gather.8
  286.7 70.4 all-gather.12
  495.1 139.5 all-reduce.5
  640.0 275.7 all-reduce.3
where the time goes:
time: 929 us; the launch traced here: 928 us
  waiting for transfers between devices  738 us (79%)
  matrix products  112 us (12%)
  local copies, waits for them, and re-layouts  49.6 us (5%)
  between operations  15.6 us (2%)
  other arithmetic  10.7 us (1%)
    psum x1, waiting for transfers between devices, local(): out_grad = lax.psum(mix_term, ('section', 'ray', 'dp'))  273 us
    psum x1, waiting for transfers between devices, spread_2(): return lax.psum(jnp.where(mine, value, jnp.zeros_like(value)), axis)  110 us
    all_gather x1, waiting for transfers between devices, local(): lax.all_gather(jnp.dot(latent, flat_pairs, preferred_element_type=jnp.flo...  66.2 us
    unnamed x12, waiting for transfers between devices  53.9 us
    all_gather x1, waiting for transfers between devices, local(): lax.all_gather(dec_out, 'section', axis=0, tiled=True)  51.5 us
    all_gather x1, waiting for transfers between devices, local(): lax.all_gather(normed, 'ray', axis=0, tiled=True)  42.5 us
    reduce_scatter x1, waiting for transfers between devices, local(): lax.psum_scatter(jnp.dot(mixed, w_attn_out, preferred_element_type=jnp.fl...  39.7 us
    all_gather x1, waiting for transfers between devices, local(): lax.all_gather(layer_norm(hidden, gain_two).astype(jnp.bfloat16), 'ray',...  39.2 us
  transfers between devices with their start and end apart: 12, of which 11 were waited for; matrix products, arithmetic and copies ran while one was open for 16% of the time, Pallas kernels for 0%

commit v1 on v0

--- a/solution.py
+++ b/solution.py
@@ -1,3 +1,4 @@
+import functools
 import math
 import jax
 import jax.numpy as jnp
@@ -5,6 +6,27 @@
 from jax.sharding import PartitionSpec as P
 
 HEADS = 16
+
+
+def rest_spans(array_in, mesh_dim):
+    o_now = lax.axis_size(mesh_dim)
+    carry = lax.axis_index(mesh_dim)
+    latest, b_now, val = (o_now, carry, array_in.shape[0])
+    seen = [dev_j * latest if src_i == 0 else dev_j for src_i, dev_j in enumerate(array_in.shape)]
+    opened = jnp.zeros(seen, array_in.dtype)
+    long_array = lax.dynamic_update_slice_in_dim(opened, array_in, b_now * val, axis=0)
+    for i0 in range(1, latest):
+        kept_arr = range(latest)
+        field_out = map(lambda src_i: (src_i, (src_i + 1) % latest), kept_arr)
+        raw_out = list(field_out)
+        array_in = lax.ppermute(array_in, mesh_dim, raw_out)
+        long_array = lax.dynamic_update_slice_in_dim(
+            long_array, array_in, (b_now - i0) % latest * val, axis=0
+        )
+    return long_array
+
+
+mark_the_shifts_all = functools.partial(rest_spans, mesh_dim="ray")
 
 
 def shifted(value, axis, by):
@@ -128,11 +150,8 @@
     queries = ray_queries[0]
     cotangent = feature_grad[0]
     flat_pairs = w_pairs.reshape(width, 2 * width)
-    key_values = lax.all_gather(
-        jnp.dot(latent, flat_pairs, preferred_element_type=jnp.float32).astype(jnp.bfloat16),
-        "ray",
-        axis=0,
-        tiled=True,
+    key_values = mark_the_shifts_all(
+        jnp.dot(latent, flat_pairs, preferred_element_type=jnp.float32).astype(jnp.bfloat16)
     )
     scene_len = key_values.shape[0]
     ray_rows = queries.shape[0]

time: 929 us -> 912 us (0.982)
  waiting for transfers between devices: 738 us -> 706 us
  local copies, waits for them, and re-layouts: 49.6 us -> 60.8 us
    all_gather x1 -> x0, waiting for transfers between devices: 66.2 us -> none  [local(): lax.all_gather(jnp.dot(latent, flat_pairs, preferred_element_type=jnp.flo...]
    ppermute x0 -> x7, waiting for transfers between devices: none -> 60.3 us  [rest_spans(): array_in = lax.ppermute(array_in, mesh_dim, raw_out)]
    all_gather x1, waiting for transfers between devices: 39.2 us -> 0.9 us  [local(): lax.all_gather(layer_norm(hidden, gain_two).astype(jnp.bfloat16), 'ray',...]
    all_gather x1, waiting for transfers between devices: 18.6 us -> 47.3 us  [local(): lax.all_gather(dec_kv, 'section', axis=0, tiled=True)]
    all_gather x1, waiting for transfers between devices: 51.5 us -> 27.2 us  [local(): lax.all_gather(dec_out, 'section', axis=0, tiled=True)]
    all_gather x1, waiting for transfers between devices: 39 us -> 49.7 us  [local(): lax.all_gather(dec_query, 'section', axis=0, tiled=True)]
    unnamed x12 -> x11, waiting for transfers between devices: 53.9 us -> 55.6 us
  transfers between devices with their start and end apart: 12 -> 18, of which waited for: 11 -> 15; matrix products, arithmetic and copies ran while one was open for 16% -> 19% of each run, Pallas kernels for 0% -> 0%
where the time goes in v1:
time: 912 us; the launch traced here: 911 us
  waiting for transfers between devices  706 us (77%)
  matrix products  112 us (12%)
  local copies, waits for them, and re-layouts  60.8 us (7%)
  between operations  14.5 us (2%)
  other arithmetic  10.7 us (1%)
    psum x1, waiting for transfers between devices, local(): out_grad = lax.psum(mix_term, ('section', 'ray', 'dp'))  273 us
    psum x1, waiting for transfers between devices, spread_2(): return lax.psum(jnp.where(mine, value, jnp.zeros_like(value)), axis)  111 us
    ppermute x7, waiting for transfers between devices, rest_spans(): array_in = lax.ppermute(array_in, mesh_dim, raw_out)  60.3 us
    unnamed x11, waiting for transfers between devices  55.6 us
    all_gather x1, waiting for transfers between devices, local(): lax.all_gather(dec_query, 'section', axis=0, tiled=True)  49.7 us
    all_gather x1, waiting for transfers between devices, local(): lax.all_gather(dec_kv, 'section', axis=0, tiled=True)  47.3 us
    all_gather x1, waiting for transfers between devices, local(): lax.all_gather(normed, 'ray', axis=0, tiled=True)  41.7 us
    dot_general x1, matrix products, local(): jnp.einsum('hrl,rhd->lhd', score_grad, query, preferred_element_type=jnp....  38.2 us
  transfers between devices with their start and end apart: 18, of which 15 were waited for; matrix products, arithmetic and copies ran while one was open for 19% of the time, Pallas kernels for 0%

profile of v1, /device:TPU:2, one launch (start us, length us, event | category | flops | bytes accessed | tf_op | source)
XLA Modules:
  0.0 911.2 jit_solution(8915413487746725635)
XLA Ops:
  13.7 41.7 %all-gather.6.cloned.1.call-done = bf16[1024,1024]{1,0:T(8,128)(2,1)} async-done(((bf16[128,1024]{1,0:T(8,128)(2,1)}), bf16[1024,1024]{1,0:T(8,128)(2,1)}) %all-gather.6.cloned.1.call-update) | async-done | bytes 2097168 | tf_op jit(solution)/shard_map/all_gather | solution.py:111
  58.0 4.9 fusion.97
  62.9 4.3 fusion.48
  70.5 47.3 %all-gather.10.cloned.1.call-done = bf16[1024,2,1024]{2,1,0:T(2,128)(2,1)} async-done(((bf16[64,2,1024]{2,1,0:T(2,128)(2,1)}), bf16[1024,2,1024]{2,1,0:T(2,128)(2,1)}) %all-gather.10.cloned.1.call-update) | async-done | bytes 4194320 | tf_op jit(solution)/shard_map/all_gather | solution.py:146
  117.8 11.1 %copy.64 = bf16[1024,2,1024]{0,2,1:T(8,128)(2,1)} copy(bf16[1024,2,1024]{2,1,0:T(2,128)(2,1)} %all-gather.10.cloned.1.call-done) | data formatting | bytes 8388608 | tf_op jit(solution)/shard_map/all_gather | solution.py:146
  129.0 3.9 convolution_convert_fusion
  134.5 34.4 %reduce-scatter.6.cloned.1.call-done = bf16[128,1024]{1,0:T(8,128)(2,1)} async-done(((bf16[1024,1024]{1,0:T(8,128)(2,1)}), bf16[128,1024]{1,0:T(8,128)(2,1)}) %reduce-scatter.6.cloned.1.call-update) | async-done | bytes 262160 | tf_op jit(solution)/shard_map/reduce_scatter | solution.py:114
  171.9 12.2 %collective-permute-done.2 = bf16[128,2048]{1,0:T(8,128)(2,1)} collective-permute-done((bf16[128,2048]{1,0:T(8,128)(2,1)}, bf16[128,2048]{1,0:T(8,128)(2,1)}, u32[]{:S(2)}, u32[]{:S(2)}) %collective-permute-start.2) | collective-permute-done | bytes 524320 | tf_op jit(solution)/shard_map/ppermute | solution.py:22
  184.1 12.1 %collective-permute-done.3 = bf16[128,2048]{1,0:T(8,128)(2,1)} collective-permute-done((bf16[128,2048]{1,0:T(8,128)(2,1)}, bf16[128,2048]{1,0:T(8,128)(2,1)}, u32[]{:S(2)}, u32[]{:S(2)}) %collective-permute-start.3) | collective-permute-done | bytes 524320 | tf_op jit(solution)/shard_map/ppermute | solution.py:22
  196.2 27.2 %all-gather.14.cloned.1.call-done = bf16[1024,1024]{1,0:T(8,128)(2,1)} async-done(((bf16[64,1024]{1,0:T(8,128)(2,1)}), bf16[1024,1024]{1,0:T(8,128)(2,1)}) %all-gather.14.cloned.1.call-update) | async-done | bytes 2097168 | tf_op jit(solution)/shard_map/all_gather | solution.py:147
  223.5 3.1 convolution_convert_fusion.4
  228.6 49.7 %all-gather.12.cloned.1.call-done = bf16[1024,1024]{1,0:T(8,128)(2,1)} async-done(((bf16[64,1024]{1,0:T(8,128)(2,1)}), bf16[1024,1024]{1,0:T(8,128)(2,1)}) %all-gather.12.cloned.1.call-update) | async-done | bytes 2097168 | tf_op jit(solution)/shard_map/all_gather | solution.py:145
  292.7 9.2 %collective-permute-done.5 = bf16[128,2048]{1,0:T(8,128)(2,1)S(1)} collective-permute-done((bf16[128,2048]{1,0:T(8,128)(2,1)}, bf16[128,2048]{1,0:T(8,128)(2,1)S(1)}, u32[]{:S(2)}, u32[]{:S(2)}) %collective-permute-start.5) | collective-permute-done | bytes 524320 | tf_op jit(solution)/shard_map/ppermute | solution.py:22
  306.7 21.6 %collective-permute-done.6 = bf16[128,2048]{1,0:T(8,128)(2,1)S(1)} collective-permute-done((bf16[128,2048]{1,0:T(8,128)(2,1)S(1)}, bf16[128,2048]{1,0:T(8,128)(2,1)S(1)}, u32[]{:S(2)}, u32[]{:S(2)}) %collective-permute-start.6) | collective-permute-done | bytes 524320 | tf_op jit(solution)/shard_map/ppermute | solution.py:22
  330.4 5.8 convolution_convert_fusion.1
  336.3 5.3 collective-permute-done.7
  342.7 4.1 fusion.96
  346.8 8.1 fusion.99
  354.9 9.8 %fusion.98 = (f32[16,256]{1,0:T(8,128)S(1)}, f32[16,256,1024]{2,1,0:T(8,128)}) fusion(bf16[256,16,64]{0,2,1:T(8,128)(2,1)S(1)} %bitcast.149, bf16[1024,16,64]{0,2,1:T(8,128)(2,1)} %bitcast.145), kind=kOutput, calls=%fused_computation.118 | convolution fusion | flops 549454848 | bytes 19415040 | tf_op jit(solution)/shard_map/sub | solution.py:52
  364.7 38.2 %fusion.38 = bf16[16,64,1024]{2,1,0:T(8,128)(2,1)} fusion(bf16[256,16,64]{0,2,1:T(8,128)(2,1)S(1)} %bitcast.150, f32[16,256,1024]{2,1,0:T(8,128)} %fusion.99, f32[16,256,1024]{2,1,0:T(8,128)} %get-tuple-element.18, f32[16,256]{1,0:T(8,128)S(1)} %get-tuple-element.17), kind=kOutput, calls=%fused_computation.40 | convolution fusion | flops 567284736 | bytes 36192256 | tf_op jit(solution)/shard_map/hrl,rhd->lhd/dot_general | solution.py:189
  402.9 7.1 fusion.35
  412.4 6.5 copy.80
  420.9 53.8 %reduce-scatter.10.cloned.1.call-done = bf16[128,2048]{1,0:T(8,128)(2,1)} async-done(((bf16[1024,2048]{1,0:T(8,128)(2,1)}), bf16[128,2048]{1,0:T(8,128)(2,1)}) %reduce-scatter.10.cloned.1.call-update) | async-done | bytes 524304
  477.0 8.5 fusion.42
  485.5 2.7 fusion.78
  488.3 10.0 %fusion.95 = (bf16[1024,1,1024]{2,1,0:T(2,128)(2,1)}, bf16[1024,1,1024]{2,1,0:T(2,128)(2,1)}) fusion(bf16[1024,2,1024]{2,1,0:T(2,128)(2,1)} %all-gather.10.cloned.1.call-done), kind=kLoop, calls=%fused_computation.115 | loop fusion | bytes 8388608 | tf_op jit(solution)/shard_map/slice | solution.py:71
  501.8 4.5 collective-permute-done
  506.2 111.3 %all-reduce.6.cloned.1.call-done = (bf16[128,1024]{1,0:T(8,128)(2,1)}, bf16[128,2,1024]{0,2,1:T(8,128)(2,1)}) async-done(((bf16[128,1024]{1,0:T(8,128)(2,1)}, bf16[128,2,1024]{0,2,1:T(8,128)(2,1)}), (bf16[128,1024]{1,0:T(8,128)(2,1)}, bf16[128,2,1024]{0,2,1:T(8,128)(2,1)})) %all-reduce.6.cloned.1.call-update) | async-done | bytes 786448 | tf_op jit(solution)/shard_map/psum | solution.py:40
  619.0 3.1 fusion.33
  622.2 3.9 fusion.49
  626.0 272.9 %all-reduce.4.cloned.1.call-done = f32[1024,1024]{1,0:T(8,128)} async-done(((f32[1024,1024]{1,0:T(8,128)}), f32[1024,1024]{1,0:T(8,128)}) %all-reduce.4.cloned.1.call-update) | async-done | bytes 4194320 | tf_op jit(solution)/shard_map/psum | solution.py:180
  899.6 4.8 copy.107
  (102 shorter events, 53.7 us)
Async XLA Ops:
  7.2 323.2 %copy-start = (bf16[1,512,1024]{2,1,0:T(8,128)(2,1)S(1)}, bf16[1,512,1024]{2,1,0:T(8,128)(2,1)}, u32[]{:S(2)}) copy-start(bf16[1,512,1024]{2,1,0:T(8,128)(2,1)} %param.19) | copy-start | bytes 3145732
  7.2 48.2 %all-gather.6.cloned.1.call-start = ((), (), s32[]{:S(2)}) async-start(), calls=%async_computation.3 | async-start | bytes 2359296 | tf_op jit(solution)/shard_map/all_gather | solution.py:111
  11.5 106.4 %all-gather.10.cloned.1.call-start = ((), (), s32[]{:S(2)}) async-start(), calls=%async_computation.7 | async-start | bytes 4456448 | tf_op jit(solution)/shard_map/all_gather | solution.py:146
  12.2 156.7 %reduce-scatter.6.cloned.1.call-start = ((), (), s32[]{:S(2)}) async-start(), calls=%async_computation.4 | async-start | bytes 2359296 | tf_op jit(solution)/shard_map/reduce_scatter | solution.py:114
  62.9 4.3 copy-start.11
  69.3 154.1 %all-gather.14.cloned.1.call-start = ((), (), s32[]{:S(2)}) async-start(), calls=%async_computation.9 | async-start | bytes 2228224 | tf_op jit(solution)/shard_map/all_gather | solution.py:147
  69.9 208.4 %all-gather.12.cloned.1.call-start = ((), (), s32[]{:S(2)}) async-start(), calls=%async_computation.8 | async-start | bytes 2228224 | tf_op jit(solution)/shard_map/all_gather | solution.py:145
  70.5 58.5 %copy-start.12 = (bf16[1,128,1024]{2,1,0:T(8,128)(2,1)S(1)}, bf16[1,128,1024]{2,1,0:T(8,128)(2,1)}, u32[]{:S(2)}) copy-start(bf16[1,128,1024]{2,1,0:T(8,128)(2,1)} %param.20) | copy-start | bytes 786436
  70.5 259.9 %all-gather.8.cloned.1.call-start = ((), (), s32[]{:S(2)}) async-start(), calls=%async_computation.5 | async-start | bytes 2359296 | tf_op jit(solution)/shard_map/all_gather | solution.py:123
  129.0 40.0 %copy-start.2 = (bf16[1,1,128,1024]{3,2,1,0:T(8,128)(2,1)S(1)}, bf16[1,1,128,1024]{3,2,1,0:T(8,128)(2,1)}, u32[]{:S(2)}) copy-start(bf16[1,1,128,1024]{3,2,1,0:T(8,128)(2,1)} %param.13) | copy-start | bytes 786436
  129.0 41.4 %copy-start.14 = (f32[1,1024]{1,0:T(1,128)S(1)}, f32[1,1024]{1,0:T(1,128)}, u32[]{:S(2)}) copy-start(f32[1,1024]{1,0:T(1,128)} %param.17) | copy-start | bytes 12292
  129.0 94.5 %copy-start.6 = (bf16[1,256,1024]{2,1,0:T(8,128)(2,1)S(1)}, bf16[1,256,1024]{2,1,0:T(8,128)(2,1)}, u32[]{:S(2)}) copy-start(bf16[1,256,1024]{2,1,0:T(8,128)(2,1)} %param.25) | copy-start | bytes 1572868
  132.9 145.5 %copy-start.8 = (bf16[1,256,1024]{2,1,0:T(8,128)(2,1)S(1)}, bf16[1,256,1024]{2,1,0:T(8,128)(2,1)}, u32[]{:S(2)}) copy-start(bf16[1,256,1024]{2,1,0:T(8,128)(2,1)} %param.21) | copy-start | bytes 1572868
  132.9 38.4 %collective-permute-start.1 = (bf16[128,2048]{1,0:T(8,128)(2,1)S(1)}, bf16[128,2048]{1,0:T(8,128)(2,1)}, u32[]{:S(2)}, u32[]{:S(2)}) collective-permute-start(bf16[128,2048]{1,0:T(8,128)(2,1)S(1)} %convolution_convert_fusion), channel_id=1, source_target_pairs={{0,2},{2,4},{4,6},{6,8},{8,10},{10,12},{12,14},{14,0},{1,3},{3,5},... | collective-permute-start | bytes 1572872 | tf_op jit(solution)/shard_map/ppermute | solution.py:22
  171.3 247.8 %reduce-scatter.8.cloned.1.call-start = ((), (), s32[]{:S(2)}) async-start(), calls=%async_computation.6 | async-start | bytes 2359296 | tf_op jit(solution)/shard_map/reduce_scatter | solution.py:131
  171.3 12.8 %collective-permute-start.2 = (bf16[128,2048]{1,0:T(8,128)(2,1)}, bf16[128,2048]{1,0:T(8,128)(2,1)}, u32[]{:S(2)}, u32[]{:S(2)}) collective-permute-start(bf16[128,2048]{1,0:T(8,128)(2,1)} %collective-permute-done.1), channel_id=1, source_target_pairs={{0,2},{2,4},{4,6},{6,8},{8,10},{10,12},{12,14},{14,0},{1,3},{3,5},... | collective-permute-start | bytes 1572872 | tf_op jit(solution)/shard_map/ppermute | solution.py:22
  184.1 12.1 %collective-permute-start.3 = (bf16[128,2048]{1,0:T(8,128)(2,1)}, bf16[128,2048]{1,0:T(8,128)(2,1)}, u32[]{:S(2)}, u32[]{:S(2)}) collective-permute-start(bf16[128,2048]{1,0:T(8,128)(2,1)} %collective-permute-done.2), channel_id=1, source_target_pairs={{0,2},{2,4},{4,6},{6,8},{8,10},{10,12},{12,14},{14,0},{1,3},{3,5},... | collective-permute-start | bytes 1572872 | tf_op jit(solution)/shard_map/ppermute | solution.py:22
  196.2 85.7 %collective-permute-start.4 = (bf16[128,2048]{1,0:T(8,128)(2,1)}, bf16[128,2048]{1,0:T(8,128)(2,1)}, u32[]{:S(2)}, u32[]{:S(2)}) collective-permute-start(bf16[128,2048]{1,0:T(8,128)(2,1)} %collective-permute-done.3), channel_id=1, source_target_pairs={{0,2},{2,4},{4,6},{6,8},{8,10},{10,12},{12,14},{14,0},{1,3},{3,5},... | collective-permute-start | bytes 1572872 | tf_op jit(solution)/shard_map/ppermute | solution.py:22
  281.9 20.0 %collective-permute-start.5 = (bf16[128,2048]{1,0:T(8,128)(2,1)}, bf16[128,2048]{1,0:T(8,128)(2,1)S(1)}, u32[]{:S(2)}, u32[]{:S(2)}) collective-permute-start(bf16[128,2048]{1,0:T(8,128)(2,1)} %collective-permute-done.4), channel_id=1, source_target_pairs={{0,2},{2,4},{4,6},{6,8},{8,10},{10,12},{12,14},{14,0},{1,3},{3,5},... | collective-permute-start | bytes 1572872 | tf_op jit(solution)/shard_map/ppermute | solution.py:22
  301.9 26.4 %collective-permute-start.6 = (bf16[128,2048]{1,0:T(8,128)(2,1)S(1)}, bf16[128,2048]{1,0:T(8,128)(2,1)S(1)}, u32[]{:S(2)}, u32[]{:S(2)}) collective-permute-start(bf16[128,2048]{1,0:T(8,128)(2,1)S(1)} %collective-permute-done.5), channel_id=1, source_target_pairs={{0,2},{2,4},{4,6},{6,8},{8,10},{10,12},{12,14},{14,0},{1,3},{3,5},... | collective-permute-start | bytes 1572872 | tf_op jit(solution)/shard_map/ppermute | solution.py:22
  328.6 13.0 %collective-permute-start.7 = (bf16[128,2048]{1,0:T(8,128)(2,1)S(1)}, bf16[128,2048]{1,0:T(8,128)(2,1)S(1)}, u32[]{:S(2)}, u32[]{:S(2)}) collective-permute-start(bf16[128,2048]{1,0:T(8,128)(2,1)S(1)} %collective-permute-done.6), channel_id=1, source_target_pairs={{0,2},{2,4},{4,6},{6,8},{8,10},{10,12},{12,14},{14,0},{1,3},{3,5},... | collective-permute-start | bytes 1572872 | tf_op jit(solution)/shard_map/ppermute | solution.py:22
  336.2 138.4 %reduce-scatter.10.cloned.1.call-start = ((), (), s32[]{:S(2)}) async-start(), calls=%async_computation.11 | async-start | bytes 4718592
  346.8 8.1 copy-start.10
  402.9 7.1 copy-start.5
  419.0 198.5 %all-reduce.6.cloned.1.call-start = ((), (), s32[]{:S(2)}) async-start(), calls=%async_computation.12 | async-start | bytes 1572864 | tf_op jit(solution)/shard_map/psum | solution.py:40
  476.7 8.8 copy-start.7
  476.7 422.2 %all-reduce.4.cloned.1.call-start = ((), (), s32[]{:S(2)}) async-start(), calls=%async_computation.10 | async-start | bytes 8388608 | tf_op jit(solution)/shard_map/psum | solution.py:180
  488.2 10.0 %copy-start.13 = (bf16[128,1024]{1,0:T(8,128)(2,1)S(1)}, bf16[128,1024]{1,0:T(8,128)(2,1)}, u32[]{:S(2)}) copy-start(bf16[128,1024]{1,0:T(8,128)(2,1)} %get-tuple-element.8) | copy-start | bytes 786436
  488.3 12.0 %copy-start.3 = (bf16[1024,1024]{1,0:T(8,128)(2,1)S(1)}, bf16[1024,1024]{1,0:T(8,128)(2,1)}, u32[]{:S(2)}) copy-start(bf16[1024,1024]{1,0:T(8,128)(2,1)} %all-gather.14.cloned.1.call-done) | copy-start | bytes 6291460
  488.3 12.0 %copy-start.9 = (bf16[1,256,1024]{2,1,0:T(8,128)(2,1)S(1)}, bf16[1,256,1024]{2,1,0:T(8,128)(2,1)}, u32[]{:S(2)}) copy-start(bf16[1,256,1024]{2,1,0:T(8,128)(2,1)} %param.21) | copy-start | bytes 1572868
  498.3 8.0 collective-permute-start
  898.9 5.5 copy-start.1
  (1 other events, 4.1 us)
Sparse Core Ops, SparseCore 0:
  11.6 43.7 all-gather.5
  58.2 59.6 all-gather.9
  120.4 48.5 reduce-scatter.5
  171.6 51.8 all-gather.13
  226.0 52.2 all-gather.11
  280.6 49.7 all-gather.7
  336.3 41.9 reduce-scatter.7
  419.1 55.5 reduce-scatter.9
  477.9 139.5 all-reduce.5
  622.8 276.0 all-reduce.3
